TPU v7x, 512 devices: a whole 4x4x16 slice. The times are simulated.
512 devices in a mesh: dp: 32 (over z, core), tensor: 16 (over y, x).
Axes of the slice: x: 4, y: 4, z: 16, core: 2. Of those that a mesh axis runs over, the one named last changes fastest.
Arguments:
- dout: bfloat16 [12288, 5120], P(('dp', 'tensor')), may hold values from -0.75 to 0.75
- attn_ctx: bfloat16 [12288, 5120], P('dp', 'tensor'), may hold values from -6 to 6
- mlp_hidden: bfloat16 [12288, 13824], P('dp', 'tensor'), may hold values from -6 to 6
- w_out: bfloat16 [5120, 5120], P('tensor', 'dp'), may hold values from -0.078125 to 0.078125
- w_down: bfloat16 [13824, 5120], P('tensor', 'dp'), may hold values from -0.0546875 to 0.0546875
- head_logits: float32 [40], replicated, may hold values from -2 to 3
- unit_logits: float32 [13824], P('tensor'), may hold values from -2 to 3
- head_noise: float32 [40], replicated, may hold values from 0.001 to 0.999
- unit_noise: float32 [13824], P('tensor'), may hold values from 0.001 to 0.999
- linear_mult: float32 [1], replicated, may hold values from 100 to 300
- square_mult: float32 [1], replicated, may hold values from 1 to 4
- target: float32 [1], replicated, may hold values from 40 to 70
Outputs:
- ctx_grad: bfloat16 [12288, 5120], P('dp', 'tensor')
- hidden_grad: bfloat16 [12288, 13824], P('dp', 'tensor')
- head_grad: float32 [40], replicated
- unit_grad: float32 [13824], P('tensor')
All inputs are finite; a program needn't handle non-finite values.
Results may differ from a plain program's by a relative error of at most 0.001.
Values may be sent and summed in bfloat16 or wider, within the bound.
No kernel may reach another device: no remote copies, remote signals or barrier semaphores. Data moves between devices by JAX's collectives and lax.ppermute only.
A program may use at most 64 MiB of HBM per device.

v0:
```python
import jax
import jax.numpy as jnp
from jax import lax
from jax.sharding import PartitionSpec as P

H = 40
HEAD = 128
FF = 13824
low_end = -0.1
high_end = 1.1
temper = 2.0 / 3.0


def concrete(logits, noise):
    shape_s = jax.nn.sigmoid((jnp.log(noise) - jnp.log(1.0 - noise) + logits) / temper)
    stretched = shape_s * (high_end - low_end) + low_end
    gate = jnp.clip(stretched, 0.0, 1.0)
    inside = jnp.logical_and(stretched > 0.0, stretched < 1.0)
    slope = jnp.where(
        inside, (high_end - low_end) / temper * shape_s * (1.0 - shape_s), 0.0 * shape_s
    )
    return (gate, slope)


def open_prob(logits):
    return jax.nn.sigmoid(logits - temper * jnp.log(-low_end / high_end))


def local(
    dout,
    attn_ctx,
    mlp_hidden,
    w_out,
    w_down,
    head_logits,
    unit_logits,
    head_noise,
    unit_noise,
    linear_mult,
    square_mult,
    target,
):
    head_gate, head_slope = concrete(head_logits, head_noise)
    unit_gate, unit_slope = concrete(unit_logits, unit_noise)
    col_count = attn_ctx.shape[1]
    head_total = head_logits.shape[0]
    tensor_index = lax.axis_index("tensor")
    columns = tensor_index * col_count + lax.iota(jnp.int32, col_count)
    owner = columns // HEAD
    member = (owner[:, None] == lax.iota(jnp.int32, head_total)[None, :]).astype(jnp.float32)
    col_gate = jnp.dot(member, head_gate, precision=lax.Precision.HIGHEST)
    full_rows = lax.all_gather(dout, "tensor", axis=0, tiled=True)
    dims = (((1,), (1,)), ((), ()))

    def contract(piece):
        return lax.dot_general(full_rows, piece, dims, preferred_element_type=jnp.float32)

    ctx_pre = contract(lax.all_gather(w_out, "dp", axis=1, tiled=True))
    hid_pre = contract(lax.all_gather(w_down, "dp", axis=1, tiled=True))
    ctx_grad = (ctx_pre * col_gate[None, :]).astype(jnp.bfloat16)
    hidden_grad = (hid_pre * unit_gate[None, :]).astype(jnp.bfloat16)
    col_part = jnp.sum(attn_ctx.astype(jnp.float32) * ctx_pre, axis=0)
    unit_part = jnp.sum(mlp_hidden.astype(jnp.float32) * hid_pre, axis=0)
    head_part = jnp.dot(col_part, member, precision=lax.Precision.HIGHEST)
    p_head = open_prob(head_logits)
    p_unit = open_prob(unit_logits)
    local_mass = jnp.sum(p_unit)
    unit_data = lax.psum(unit_part, "dp")
    head_data = lax.psum(head_part, ("dp", "tensor"))
    unit_mass = lax.psum(local_mass, "tensor")
    denom = 4.0 * HEAD * H + 3.0 * FF
    size = 100.0 * (4.0 * HEAD * jnp.sum(p_head) + 3.0 * unit_mass) / denom
    factor = linear_mult[0] + 2.0 * square_mult[0] * (size - target[0])
    head_grad = head_data * head_slope + factor * (400.0 * HEAD / denom) * p_head * (1.0 - p_head)
    unit_grad = unit_data * unit_slope + factor * (300.0 / denom) * p_unit * (1.0 - p_unit)
    return (ctx_grad, hidden_grad, head_grad, unit_grad)


def solution(mesh):
    placed = (
        P(("dp", "tensor"), None),
        P("dp", "tensor"),
        P("dp", "tensor"),
        P("tensor", "dp"),
        P("tensor", "dp"),
        P(),
        P("tensor"),
        P(),
        P("tensor"),
        P(),
        P(),
        P(),
    )
    return jax.shard_map(
        local,
        mesh=mesh,
        in_specs=placed,
        out_specs=(P("dp", "tensor"), P("dp", "tensor"), P(), P("tensor")),
        check_vma=False,
    )
```

profile of v0, /device:TPU:1, one launch (start us, length us, event | category | flops | bytes accessed | tf_op | source)
XLA Modules:
  0.0 329.6 jit_solution(5489138382124432926)
XLA Ops:
  7.2 0.0 all-gather.6.cloned.1.call-start
  7.2 0.7 all-gather.6.cloned.1.call-update
  7.9 0.0 all-gather.4.cloned.1.call-start
  7.9 0.7 all-gather.4.cloned.1.call-update
  8.6 0.0 all-gather.8.cloned.1.call-start
  8.7 0.7 all-gather.8.cloned.1.call-update
  9.4 1.3 fusion.2
  10.7 34.9 %psum.22 = f32[]{:T(128)} all-reduce(f32[]{:T(128)} %get-tuple-element.11), channel_id=1, replica_groups=mesh['dp'=32,'tensor'=16] {'tensor'}, use_global_device_ids=true, to_apply=%region_4.5 | all-reduce | flops 1 | bytes 8 | tf_op jit(solution)/shard_map/psum | solution.py:70
  48.2 1.3 fusion.17
  50.1 0.0 copy-start.2
  50.1 0.0 copy-start.3
  50.2 0.0 copy-start.4
  50.2 38.7 %all-gather.6.cloned.1.call-done = bf16[320,5120]{0,1:T(8,128)(2,1)} async-done(((bf16[320,160]{0,1:T(8,128)(2,1)}), bf16[320,5120]{0,1:T(8,128)(2,1)}) %all-gather.6.cloned.1.call-update) | async-done | bytes 3276816 | tf_op jit(solution)/shard_map/all_gather | solution.py:58
  88.8 65.0 %all-gather.4.cloned.1.call-done = bf16[384,5120]{1,0:T(8,128)(2,1)} async-done(((bf16[24,5120]{1,0:T(8,128)(2,1)}), bf16[384,5120]{1,0:T(8,128)(2,1)}) %all-gather.4.cloned.1.call-update) | async-done | bytes 3932176 | tf_op jit(solution)/shard_map/all_gather | solution.py:52
  153.9 5.3 %multiply_reduce_fusion.1 = (f32[320]{0:T(512)S(1)}, f32[384,320]{0,1:T(8,128)S(1)}) fusion(bf16[384,320]{0,1:T(8,128)(2,1)} %param.13, bf16[384,5120]{1,0:T(8,128)(2,1)} %all-gather.4.cloned.1.call-done, bf16[320,5120]{0,1:T(8,128)(2,1)} %all-gather.6.cloned.1.call-done), kind=kOutput, calls=%fused_computation.4 | convolution fusion | flops 1258659584 | bytes 7947520 | tf_op jit(solution)/shard_map/dot_general | solution.py:56
  159.2 0.2 convolution_bitcast_fusion
  159.5 105.0 %psum.21 = f32[40]{0:T(128)S(1)} all-reduce(f32[40]{0:T(128)S(1)} %convolution_bitcast_fusion), channel_id=1, replica_groups=mesh['dp'=32,'tensor'=16] {'dp','tensor'}, use_global_device_ids=true, to_apply=%region_1.2 | all-reduce | flops 40 | bytes 320 | tf_op jit(solution)/shard_map/psum | solution.py:69
  264.5 0.0 copy-done.2
  264.5 0.0 copy-done.3
  264.5 0.5 multiply_add_fusion.2
  265.0 0.3 convolution_reduce_fusion
  265.3 0.8 multiply_convert_fusion.1
  266.1 0.0 all-gather.8.cloned.1.call-done
  266.2 0.0 copy-done.4
  266.2 0.0 copy-start
  266.2 0.0 copy-start.1
  266.2 10.5 %multiply_reduce_fusion = (f32[864]{0:T(1024)S(1)}, bf16[384,864]{0,1:T(8,128)(2,1)}) fusion(bf16[384,864]{0,1:T(8,128)(2,1)S(1)} %copy-done.4, f32[864]{0:T(1024)S(1)} %get-tuple-element.10, bf16[384,5120]{1,0:T(8,128)(2,1)} %all-gather.4.cloned.1.call-done, bf16[864,5120]{0,1:T(8,128)(2,1)} %all-gather.8.cloned.1.call-done), kind=kOutput, calls=%fused_computation | convolution fusion | flops 3399044352 | bytes 14113536 | tf_op jit(solution)/shard_map/dot_general | solution.py:56
  276.7 45.8 %psum.23 = f32[864]{0:T(1024)S(1)} all-reduce(f32[864]{0:T(1024)S(1)} %get-tuple-element.8), channel_id=1, replica_groups=mesh['dp'=32,'tensor'=16] {'dp'}, use_global_device_ids=true, to_apply=%region_6.7 | all-reduce | flops 864 | bytes 6912 | tf_op jit(solution)/shard_map/psum | solution.py:68
  322.5 0.0 copy-done
  322.5 0.0 copy-done.1
  322.5 0.6 multiply_add_fusion
  (2 shorter events, 0.0 us)
Async XLA Ops:
  7.2 81.7 %all-gather.6.cloned.1.call-start = ((), (), s32[]{:S(2)}) async-start(), calls=%async_computation.1 | async-start | bytes 4055040 | tf_op jit(solution)/shard_map/all_gather | solution.py:58
  7.9 146.0 %all-gather.4.cloned.1.call-start = ((), (), s32[]{:S(2)}) async-start(), calls=%async_computation | async-start | bytes 4177920 | tf_op jit(solution)/shard_map/all_gather | solution.py:52
  8.6 257.5 %all-gather.8.cloned.1.call-start = ((), (), s32[]{:S(2)}) async-start(), calls=%async_computation.2 | async-start | bytes 9461760 | tf_op jit(solution)/shard_map/all_gather | solution.py:59
  50.1 214.4 %copy-start.2 = (f32[40]{0:T(128)S(1)}, f32[40]{0:T(128)}, u32[]{:S(2)}) copy-start(f32[40]{0:T(128)} %param.17) | copy-start | bytes 484
  50.1 214.4 %copy-start.3 = (f32[40]{0:T(128)S(1)}, f32[40]{0:T(128)}, u32[]{:S(2)}) copy-start(f32[40]{0:T(128)} %param.19) | copy-start | bytes 484
  50.2 216.0 %copy-start.4 = (bf16[384,864]{0,1:T(8,128)(2,1)S(1)}, bf16[384,864]{0,1:T(8,128)(2,1)}, u32[]{:S(2)}) copy-start(bf16[384,864]{0,1:T(8,128)(2,1)} %param.14) | copy-start | bytes 1990660
  266.2 56.3 %copy-start = (f32[864]{0:T(1024)S(1)}, f32[864]{0:T(1024)}, u32[]{:S(2)}) copy-start(f32[864]{0:T(1024)} %param.18) | copy-start | bytes 10372
  266.2 56.3 %copy-start.1 = (f32[864]{0:T(1024)S(1)}, f32[864]{0:T(1024)}, u32[]{:S(2)}) copy-start(f32[864]{0:T(1024)} %param.20) | copy-start | bytes 10372
Sparse Core Ops, SparseCore 0:
  10.1 78.6 all-gather.5
  91.8 61.9 all-gather.3
  156.0 80.5 all-gather.7
where the time goes:
time: 330 us
  blocking collectives  186 us (56%)
  waiting for transfers between devices  106 us (32%)
  between operations  17.1 us (5%)
  matrix products  16.4 us (5%)
  other arithmetic  4.6 us (1%)
    psum x1, blocking collectives, local(): head_data = lax.psum(head_part, ('dp', 'tensor'))  105 us
    all_gather x1, waiting for transfers between devices, local(): full_rows = lax.all_gather(dout, 'tensor', axis=0, tiled=True)  65 us
    psum x1, blocking collectives, local(): unit_data = lax.psum(unit_part, 'dp')  45.8 us
    all_gather x1, waiting for transfers between devices, local(): ctx_pre = contract(lax.all_gather(w_out, 'dp', axis=1, tiled=True))  38.7 us
    psum x1, blocking collectives, local(): unit_mass = lax.psum(local_mass, 'tensor')  34.9 us
    dot_general x2, matrix products, contract(): lax.dot_general(full_rows, piece, dims, preferred_element_type=jnp.float32)  15.9 us
  transfers between devices with their start and end apart: 3, of which 2 were waited for; matrix products, arithmetic and copies ran while one was open for 3% of the time, Pallas kernels for 0%

commit v1 on v0

--- a/solution.py
+++ b/solution.py
@@ -66,7 +66,13 @@
     p_unit = open_prob(unit_logits)
     local_mass = jnp.sum(p_unit)
     unit_data = lax.psum(unit_part, "dp")
-    head_data = lax.psum(head_part, ("dp", "tensor"))
+
+    def drive_lots_all(unit):
+        for hop_no in ("tensor", "dp"):
+            unit = lax.psum(unit, axis_name=hop_no)
+        return unit
+
+    head_data = drive_lots_all(head_part)
     unit_mass = lax.psum(local_mass, "tensor")
     denom = 4.0 * HEAD * H + 3.0 * FF
     size = 100.0 * (4.0 * HEAD * jnp.sum(p_head) + 3.0 * unit_mass) / denom

time: 330 us -> 303 us (0.918)
  blocking collectives: 186 us -> 78.2 us
  waiting for transfers between devices: 106 us -> 185 us
    psum x3 -> x2, blocking collectives: 186 us -> 78.2 us  [drive_lots_all(): unit = lax.psum(unit, axis_name=hop_no)]
    all_gather x1, waiting for transfers between devices: 0.01 us -> 43.7 us  [local(): hid_pre = contract(lax.all_gather(w_down, 'dp', axis=1, tiled=True))]
    all_gather x1, waiting for transfers between devices: 38.7 us -> 74.3 us  [local(): ctx_pre = contract(lax.all_gather(w_out, 'dp', axis=1, tiled=True))]
  transfers between devices with their start and end apart: 3 -> 3, of which waited for: 2 -> 3; matrix products, arithmetic and copies ran while one was open for 3% -> 3% of each run, Pallas kernels for 0% -> 0%
where the time goes in v1:
time: 303 us; the launch traced here: 301 us
  waiting for transfers between devices  185 us (61%)
  blocking collectives  78.2 us (26%)
  between operations  17.1 us (6%)
  matrix products  16.4 us (5%)
  other arithmetic  4.6 us (2%)
    psum x2, blocking collectives, drive_lots_all(): unit = lax.psum(unit, axis_name=hop_no)  78.2 us
    all_gather x1, waiting for transfers between devices, local(): ctx_pre = contract(lax.all_gather(w_out, 'dp', axis=1, tiled=True))  74.3 us
    all_gather x1, waiting for transfers between devices, local(): full_rows = lax.all_gather(dout, 'tensor', axis=0, tiled=True)  64.8 us
    all_gather x1, waiting for transfers between devices, local(): hid_pre = contract(lax.all_gather(w_down, 'dp', axis=1, tiled=True))  43.7 us
    dot_general x2, matrix products, contract(): lax.dot_general(full_rows, piece, dims, preferred_element_type=jnp.float32)  15.9 us
  transfers between devices with their start and end apart: 3, of which 3 were waited for; matrix products, arithmetic and copies ran while one was open for 3% of the time, Pallas kernels for 0%

profile of v1, /device:TPU:1, one launch (start us, length us, event | category | flops | bytes accessed | tf_op | source)
XLA Modules:
  0.0 301.3 jit_solution(986423120768863830)
XLA Ops:
  7.2 0.0 all-gather.6.cloned.1.call-start
  7.2 0.7 all-gather.6.cloned.1.call-update
  7.9 0.0 all-gather.4.cloned.1.call-start
  7.9 0.7 all-gather.4.cloned.1.call-update
  8.6 0.0 all-gather.8.cloned.1.call-start
  8.7 0.7 all-gather.8.cloned.1.call-update
  11.3 1.3 fusion.17
  13.3 1.3 fusion.2
  14.6 0.0 copy-start.4
  14.6 74.3 %all-gather.6.cloned.1.call-done = bf16[320,5120]{0,1:T(8,128)(2,1)} async-done(((bf16[320,160]{0,1:T(8,128)(2,1)}), bf16[320,5120]{0,1:T(8,128)(2,1)}) %all-gather.6.cloned.1.call-update) | async-done | bytes 3276816 | tf_op jit(solution)/shard_map/all_gather | solution.py:58
  88.9 64.8 %all-gather.4.cloned.1.call-done = bf16[384,5120]{1,0:T(8,128)(2,1)} async-done(((bf16[24,5120]{1,0:T(8,128)(2,1)}), bf16[384,5120]{1,0:T(8,128)(2,1)}) %all-gather.4.cloned.1.call-update) | async-done | bytes 3932176 | tf_op jit(solution)/shard_map/all_gather | solution.py:52
  153.7 5.3 %multiply_reduce_fusion.1 = (f32[320]{0:T(512)S(1)}, f32[384,320]{0,1:T(8,128)S(1)}) fusion(bf16[384,320]{0,1:T(8,128)(2,1)} %param.13, bf16[384,5120]{1,0:T(8,128)(2,1)} %all-gather.4.cloned.1.call-done, bf16[320,5120]{0,1:T(8,128)(2,1)} %all-gather.6.cloned.1.call-done), kind=kOutput, calls=%fused_computation.4 | convolution fusion | flops 1258659584 | bytes 7947520 | tf_op jit(solution)/shard_map/dot_general | solution.py:56
  159.1 0.2 convolution_bitcast_fusion
  159.3 31.8 %all-reduce.1 = (f32[40]{0:T(128)S(1)}, f32[]{:T(128)}) all-reduce(f32[40]{0:T(128)S(1)} %convolution_bitcast_fusion, f32[]{:T(128)} %get-tuple-element.15), channel_id=1, replica_groups=mesh['dp'=32,'tensor'=16] {'tensor'}, use_global_device_ids=true, to_apply=%region_1.2 | all-reduce | flops 41 | bytes 328 | tf_op jit(solution)/shard_map/psum | solution.py:72
  191.8 43.7 %all-gather.8.cloned.1.call-done = bf16[864,5120]{0,1:T(8,128)(2,1)} async-done(((bf16[864,160]{0,1:T(8,128)(2,1)}), bf16[864,5120]{0,1:T(8,128)(2,1)}) %all-gather.8.cloned.1.call-update) | async-done | bytes 8847376 | tf_op jit(solution)/shard_map/all_gather | solution.py:59
  235.5 0.0 copy-done.4
  235.5 0.0 copy-start.2
  235.5 0.0 copy-start.3
  235.5 0.0 copy-start
  235.5 0.0 copy-start.1
  235.5 10.5 %multiply_convert_fusion = (bf16[384,864]{0,1:T(8,128)(2,1)}, f32[864]{0:T(1024)S(1)}) fusion(f32[864]{0:T(1024)S(1)} %get-tuple-element.14, bf16[384,864]{0,1:T(8,128)(2,1)S(1)} %copy-done.4, bf16[384,5120]{1,0:T(8,128)(2,1)} %all-gather.4.cloned.1.call-done, bf16[864,5120]{0,1:T(8,128)(2,1)} %all-gather.8.cloned.1.call-done), kind=kOutput, calls=%fused_computation.1 | convolution fusion | flops 3399044352 | bytes 14113536 | tf_op jit(solution)/shard_map/dot_general | solution.py:56
  246.1 46.4 %all-reduce = (f32[40]{0:T(128)S(1)}, f32[864]{0:T(1024)S(1)}) all-reduce(f32[40]{0:T(128)S(1)} %get-tuple-element.6, f32[864]{0:T(1024)S(1)} %get-tuple-element.13), channel_id=1, replica_groups=mesh['dp'=32,'tensor'=16] {'dp'}, use_global_device_ids=true, to_apply=%region_2.3 | all-reduce | flops 904 | bytes 7232 | tf_op jit(solution)/shard_map/psum | solution.py:72
  292.4 0.0 copy-done.2
  292.4 0.0 copy-done.3
  292.5 0.5 multiply_add_fusion.2
  293.0 0.3 convolution_reduce_fusion
  293.3 0.8 multiply_convert_fusion.1
  294.1 0.0 copy-done
  294.1 0.0 copy-done.1
  294.1 0.6 multiply_add_fusion
  (2 shorter events, 0.0 us)
Async XLA Ops:
  7.2 81.8 %all-gather.6.cloned.1.call-start = ((), (), s32[]{:S(2)}) async-start(), calls=%async_computation.1 | async-start | bytes 4055040 | tf_op jit(solution)/shard_map/all_gather | solution.py:58
  7.9 145.8 %all-gather.4.cloned.1.call-start = ((), (), s32[]{:S(2)}) async-start(), calls=%async_computation | async-start | bytes 4177920 | tf_op jit(solution)/shard_map/all_gather | solution.py:52
  8.6 226.9 %all-gather.8.cloned.1.call-start = ((), (), s32[]{:S(2)}) async-start(), calls=%async_computation.2 | async-start | bytes 9461760 | tf_op jit(solution)/shard_map/all_gather | solution.py:59
  14.6 220.9 %copy-start.4 = (bf16[384,864]{0,1:T(8,128)(2,1)S(1)}, bf16[384,864]{0,1:T(8,128)(2,1)}, u32[]{:S(2)}) copy-start(bf16[384,864]{0,1:T(8,128)(2,1)} %param.14) | copy-start | bytes 1990660
  235.5 56.9 %copy-start.2 = (f32[40]{0:T(128)S(1)}, f32[40]{0:T(128)}, u32[]{:S(2)}) copy-start(f32[40]{0:T(128)} %param.17) | copy-start | bytes 484
  235.5 56.9 %copy-start.3 = (f32[40]{0:T(128)S(1)}, f32[40]{0:T(128)}, u32[]{:S(2)}) copy-start(f32[40]{0:T(128)} %param.19) | copy-start | bytes 484
  235.5 58.6 %copy-start = (f32[864]{0:T(1024)S(1)}, f32[864]{0:T(1024)}, u32[]{:S(2)}) copy-start(f32[864]{0:T(1024)} %param.18) | copy-start | bytes 10372
  235.5 58.6 %copy-start.1 = (f32[864]{0:T(1024)S(1)}, f32[864]{0:T(1024)}, u32[]{:S(2)}) copy-start(f32[864]{0:T(1024)} %param.20) | copy-start | bytes 10372
Sparse Core Ops, SparseCore 0:
  10.1 78.7 all-gather.5
  91.9 61.7 all-gather.3
  155.9 79.6 all-gather.7
